TPU v7x, 256 devices: a whole 4x4x8 slice. The times are simulated.
256 devices in a mesh: st: 16 (over y, x), tp: 16 (over z, core).
Axes of the slice: x: 4, y: 4, z: 8, core: 2. Of those that a mesh axis runs over, the one named last changes fastest.
Arguments:
- continuous: bfloat16 [512, 3, 1424], P(('st', 'tp')), may hold values from -48 to 48
- templates: bfloat16 [512, 12, 3, 400], P(('st', 'tp')), may hold values from -120 to 120
- station_list: int32 [512, 12], P(('st', 'tp')), may hold values from 0 to 511, as said below
- moveouts: int32 [512, 12], P(('st', 'tp')), may hold values from 0 to 256
Outputs:
- detection: float32 [512, 768], P(('st', 'tp'))
Inputs may be any that keep to these rules, and one draw needn't show every extreme that they name: `station_list`: A station's group is station // 32. The 12 stations of a template are distinct, and so are their indices within their groups (station % 32). The rows of one device (2 templates, aligned blocks in order) name at most 3 stations of any one group, and in every such block one group is named exactly 3 times; blocks b and b2 with b % 16 == b2 % 16 share that group.
All inputs are finite; a program needn't handle non-finite values.
Results may differ from a plain program's by a relative error of at most 0.0003.
Values may be sent and summed in bfloat16 or wider, within the bound.
No kernel may reach another device: no remote copies, remote signals or barrier semaphores. Data moves between devices by JAX's collectives and lax.ppermute only.
A program may use at most 64 MiB of HBM per device.

v0:
```python
import math
import jax
import jax.numpy as jnp
from jax import lax
from jax.sharding import PartitionSpec as P

WIN = 768
TLEN = 400
CH = 3
OUT = 1024
EPS = 1e-05


def frame_width():
    return 128


def toeplitz(vector, row_width, frame_size):
    leading = vector.shape[:-1]
    padded = jnp.concatenate(
        [vector, jnp.zeros(leading + (row_width + 1 - vector.shape[-1],), vector.dtype)], axis=-1
    )
    repeated = jnp.tile(padded, (1,) * len(leading) + (frame_size,))
    return repeated[..., : frame_size * row_width].reshape(leading + (frame_size, row_width))


def to_frames(series, frame_size, frame_count):
    target = frame_size * frame_count
    length_now = series.shape[-1]
    if length_now >= target:
        fitted = series[..., :target]
    else:
        fitted = jnp.concatenate(
            [series, jnp.zeros(series.shape[:-1] + (target - length_now,), series.dtype)], axis=-1
        )
    return fitted.reshape(series.shape[:-1] + (frame_count, frame_size))


def inverse_level(row_data):
    squares = jnp.square(row_data.astype(jnp.float32))
    running = jnp.cumsum(squares, axis=-1)
    running = jnp.concatenate([jnp.zeros(running.shape[:-1] + (1,), jnp.float32), running], axis=-1)
    energy = running[..., TLEN : TLEN + OUT] - running[..., :OUT]
    return lax.rsqrt(energy / TLEN + EPS)


def correlate(templates, row_data, inverse, shifts):
    frame_size = frame_width()
    blocks = OUT // frame_size
    step_count = (TLEN + 2 * frame_size - 2) // frame_size
    frames = to_frames(row_data, frame_size, blocks + step_count - 1)
    bands = toeplitz(templates, step_count * frame_size, frame_size)
    running = jnp.zeros(templates.shape[:-1] + (blocks, frame_size), jnp.float32)
    for step_index in range(step_count):
        running = running + jnp.einsum(
            "ncbp,ncip->ncbi",
            frames[:, :, step_index : step_index + blocks],
            bands[..., step_index * frame_size : (step_index + 1) * frame_size],
            preferred_element_type=jnp.float32,
        )
    raw_sums = running.reshape(templates.shape[:-1] + (OUT,))
    template_values = templates.astype(jnp.float32)
    template_inverse = lax.rsqrt(jnp.mean(template_values * template_values, axis=-1) + EPS)
    scaled = raw_sums * inverse * (template_inverse / TLEN)[..., None]
    summed = jnp.sum(scaled, axis=1)
    return jax.vmap(lambda series, start_at: lax.dynamic_slice_in_dim(series, start_at, WIN))(
        summed, shifts
    )


def in_blocks(worker, arrays, item_count):
    block_size = math.gcd(item_count, 32)
    grouped = jax.tree.map(
        lambda member: member.reshape((item_count // block_size, block_size) + member.shape[1:]),
        arrays,
    )
    result = lax.map(worker, grouped)
    return result.reshape((item_count,) + result.shape[2:])


def shards(continuous, templates, station_list, moveouts):
    group_count = lax.axis_size("st")
    template_count = templates.shape[0]
    list_size = templates.shape[1]
    group_size = continuous.shape[0] * lax.axis_size("tp")
    entries = template_count * list_size
    capacity = 2 * entries // group_count
    slots_total = group_count * capacity
    flat_list = station_list.reshape(entries)
    owners = flat_list // group_size
    within = flat_list - owners * group_size
    member = (owners[:, None] == jnp.arange(group_count, dtype=jnp.int32)[None, :]).astype(
        jnp.int32
    )
    earlier = jnp.cumsum(member, axis=0) - member
    position = jnp.sum(earlier * member, axis=1)
    slot_index = owners * capacity + position
    flat_shift = moveouts.reshape(entries)
    flat_templates = templates.reshape(entries, CH, TLEN)
    group_rows = lax.all_gather(continuous, "tp", axis=0, tiled=True)
    local_scale = inverse_level(continuous)
    group_scale = lax.all_gather(local_scale, "tp", axis=0, tiled=True)
    slot_templates = (
        jnp.zeros((slots_total, CH, TLEN), jnp.bfloat16)
        .at[slot_index]
        .set(flat_templates)
        .reshape(group_count, capacity, CH, TLEN)
    )
    slot_station = (
        jnp.zeros((slots_total,), jnp.int32)
        .at[slot_index]
        .set(within)
        .reshape(group_count, capacity)
    )
    slot_shift = (
        jnp.zeros((slots_total,), jnp.int32)
        .at[slot_index]
        .set(flat_shift)
        .reshape(group_count, capacity)
    )
    template_rows = jnp.arange(entries, dtype=jnp.int32) // list_size
    slot_row = (
        jnp.full((slots_total,), -1, jnp.int32)
        .at[slot_index]
        .set(template_rows)
        .reshape(group_count, capacity)
    )
    pieces = (
        lax.all_to_all(slot_templates, "st", split_axis=0, concat_axis=0, tiled=True),
        lax.all_to_all(slot_station, "st", split_axis=0, concat_axis=0, tiled=True),
        lax.all_to_all(slot_shift, "st", split_axis=0, concat_axis=0, tiled=True),
        lax.all_to_all(slot_row, "st", split_axis=0, concat_axis=0, tiled=True),
    )
    given_items = pieces[1].shape[1]
    item_total = group_count * given_items
    stations = pieces[1].reshape(item_total)

    def block_work(block_parts):
        picked = group_rows[block_parts[1]]
        scales = group_scale[block_parts[1]]
        return correlate(block_parts[0], picked, scales, block_parts[2])

    aligned = in_blocks(
        block_work,
        (pieces[0].reshape(item_total, CH, TLEN), stations, pieces[2].reshape(item_total)),
        item_total,
    )
    aligned = aligned.reshape(group_count, given_items, WIN)
    outcome = lax.all_to_all(aligned, "st", split_axis=0, concat_axis=0, tiled=True)
    returned = outcome.reshape(slots_total, WIN)
    detection = jnp.sum(returned[slot_index].reshape(template_count, list_size, WIN), axis=1)
    return detection


def solution(mesh):
    placed = (
        P(("st", "tp"), None, None),
        P(("st", "tp"), None, None, None),
        P(("st", "tp"), None),
        P(("st", "tp"), None),
    )
    return jax.shard_map(
        shards, mesh=mesh, in_specs=placed, out_specs=P(("st", "tp"), None), check_vma=False
    )
```

profile of v0, /device:TPU:1, one launch (start us, length us, event | category | flops | bytes accessed | tf_op | source)
XLA Modules:
  0.0 315.8 jit_solution(9241197503857095357)
XLA Ops:
  3.2 7.6 %all-to-all-start = ((s32[16,1,3]{2,1,0:T(1,128)}), s32[16,1,3]{2,1,0:T(1,128)S(1)}, u32[]{:S(2)}, u32[]{:S(2)}) async-start(s32[16,1,3]{2,1,0:T(1,128)} %bitcast.7), calls=%async_computation | async-start | bytes 16384 | tf_op jit(solution)/shard_map/all_to_all | solution.py:130
  13.8 1.7 reduce-window.6
  16.6 22.2 %all_gather.7 = f32[32,3,1024]{2,1,0:T(4,128)S(1)} all-gather(f32[2,3,1024]{2,1,0:T(4,128)S(1)} %copy.76), channel_id=1, replica_groups=mesh['st'=16,'tp'=16] {'tp'}, dimensions={0}, use_global_device_ids=true | all-gather | bytes 417792 | tf_op jit(solution)/shard_map/all_gather | solution.py:102
  39.6 6.9 %all-to-all-start.2 = ((s32[16,1,3]{2,1,0:T(1,128)}), s32[16,1,3]{2,1,0:T(1,128)S(1)}, u32[]{:S(2)}, u32[]{:S(2)}) async-start(s32[16,1,3]{2,1,0:T(1,128)} %bitcast.11), calls=%async_computation.2 | async-start | bytes 16384 | tf_op jit(solution)/shard_map/all_to_all | solution.py:131
  46.6 1.5 scatter_fusion
  48.9 3.9 %all-to-all-done.2 = s32[16,1,3]{2,1,0:T(1,128)S(1)} async-done(((s32[16,1,3]{2,1,0:T(1,128)}), s32[16,1,3]{2,1,0:T(1,128)S(1)}, u32[]{:S(2)}, u32[]{:S(2)}) %all-to-all-start.2) | async-done | bytes 224 | tf_op jit(solution)/shard_map/all_to_all | solution.py:131
  52.8 3.5 %all-to-all-start.1 = ((bf16[16,3,3,400]{3,1,2,0:T(4,128)(2,1)}), bf16[16,3,3,400]{3,1,2,0:T(4,128)(2,1)S(1)}, u32[]{:S(2)}, u32[]{:S(2)}) async-start(bf16[16,3,3,400]{3,1,2,0:T(4,128)(2,1)} %copy.70), calls=%async_computation.1 | async-start | bytes 393216 | tf_op jit(solution)/shard_map/all_to_all | solution.py:129
  56.3 16.9 %all_gather.6 = bf16[32,3,1424]{2,1,0:T(4,128)(2,1)S(1)} all-gather(bf16[2,3,1424]{2,1,0:T(4,128)(2,1)S(1)} %copy.67), channel_id=1, replica_groups=mesh['st'=16,'tp'=16] {'tp'}, dimensions={0}, use_global_device_ids=true | all-gather | bytes 290496 | tf_op jit(solution)/shard_map/all_gather | solution.py:100
  75.9 222.4 %while.13 = (s32[]{:T(128)}, f32[3,16,768]{2,1,0:T(8,128)}, s32[3,16]{1,0:T(4,128)S(1)}, bf16[32,3,1424]{2,1,0:T(4,128)(2,1)S(1)}, bf16[3,16,3,400]{3,1,0,2:T(8,...) while((s32[]{:T(128)}, f32[3,16,768]{2,1,0:T(8,128)}, ...), condition=%wide.region_10.11_spmd, body=%wide.region_7.10_spmd.sunk | while | flops 63301088 | bytes 91004616 | solution.py:77
  77.8 4.3 %tile.11 = bf16[16,3,128,641]{3,2,0,1:T(8,128)(2,1)} broadcast(bf16[16,3,641]{2,0,1:T(8,128)(2,1)S(1)} %concatenate.21), dimensions={0,1,3} | broadcast | bytes 7938144 | tf_op jit(solution)/shard_map/while/body/eval_jaxpr/tile | solution.py:23
  82.1 14.9 %tile.12 = bf16[16,3,82048]{2,0,1:T(8,128)(2,1)} reshape(bf16[16,3,128,641]{3,2,0,1:T(8,128)(2,1)} %tile.11) | data formatting | bytes 15753216 | tf_op jit(solution)/shard_map/while/body/eval_jaxpr/tile | solution.py:23
  97.0 3.2 %slice-done = bf16[16,3,81920]{2,0,1:T(8,128)(2,1)S(1)} async-done(((bf16[16,3,82048]{2,0,1:T(8,128)(2,1)}), bf16[16,3,81920]{2,0,1:T(8,128)(2,1)S(1)}, s32[]{:S(2)}) %slice-start) | async-done | bytes 7864344 | tf_op jit(solution)/shard_map/while/body/eval_jaxpr/slice | solution.py:24
  100.2 4.6 %copy.136 = bf16[6,8,128,640]{3,2,1,0:T(8,128)(2,1)} copy(bf16[6,8,128,640]{3,1,2,0:T(8,128)(2,1)S(1)} %bitcast.72) | data formatting | bytes 15728640 | tf_op jit(solution)/shard_map/while
  104.8 3.7 %fusion.78 = (bf16[16,3,128,128]{3,2,0,1:T(8,128)(2,1)S(1)}, bf16[16,3,128,128]{3,2,0,1:T(8,128)(2,1)S(1)}, bf16[16,3,128,128]{3,2,0,1:T(8,128)(2,1)S(1)}, bf16[...) fusion(bf16[16,3,128,640]{3,2,0,1:T(8,128)(2,1)} %bitcast.73), kind=kLoop, calls=%fused_computation.70.clone.1 | loop fusion | bytes 15728640 | tf_op jit(solution)/shard_map/while/body/eval_jaxpr/slice | solution.py:58
  114.1 35.3 %while.14 = (s32[]{:T(128)}, f32[16,1024]{1,0:T(8,128)S(1)}, s32[16,2]{0,1:T(2,128)S(1)}, f32[16,768]{1,0:T(8,128)S(1)}, s32[]{:T(128)}, /*index=5*/s32[]{:T(128)}) while((s32[]{:T(128)}, f32[16,1024]{1,0:T(8,128)S(1)}, s32[16,2]{0,1:T(2,128)S(1)}, f32[16,768]{1,0:T(8,128)S(1)}, s32[]{:T(128)}, /*index=5*/s32[]{:T(128)}) %tuple.55), condition=%wide.while_cond, body=%wide.while_body.sunk | while | flops 2 | bytes 12401 | solution.py:66
  114.8 1.5 dynamic-slice.7
  117.0 1.5 dynamic-slice.7
  119.2 1.5 dynamic-slice.7
  121.4 1.5 dynamic-slice.7
  123.6 1.5 dynamic-slice.7
  125.9 1.5 dynamic-slice.7
  128.1 1.5 dynamic-slice.7
  130.3 1.5 dynamic-slice.7
  132.5 1.5 dynamic-slice.7
  134.7 1.5 dynamic-slice.7
  136.9 1.5 dynamic-slice.7
  139.1 1.5 dynamic-slice.7
  141.3 1.5 dynamic-slice.7
  143.5 1.5 dynamic-slice.7
  145.7 1.5 dynamic-slice.7
  147.9 1.5 dynamic-slice.7
  152.0 4.3 %tile.11 = bf16[16,3,128,641]{3,2,0,1:T(8,128)(2,1)} broadcast(bf16[16,3,641]{2,0,1:T(8,128)(2,1)S(1)} %concatenate.21), dimensions={0,1,3} | broadcast | bytes 7938144 | tf_op jit(solution)/shard_map/while/body/eval_jaxpr/tile | solution.py:23
  156.2 14.9 %tile.12 = bf16[16,3,82048]{2,0,1:T(8,128)(2,1)} reshape(bf16[16,3,128,641]{3,2,0,1:T(8,128)(2,1)} %tile.11) | data formatting | bytes 15753216 | tf_op jit(solution)/shard_map/while/body/eval_jaxpr/tile | solution.py:23
  171.1 3.2 %slice-done = bf16[16,3,81920]{2,0,1:T(8,128)(2,1)S(1)} async-done(((bf16[16,3,82048]{2,0,1:T(8,128)(2,1)}), bf16[16,3,81920]{2,0,1:T(8,128)(2,1)S(1)}, s32[]{:S(2)}) %slice-start) | async-done | bytes 7864344 | tf_op jit(solution)/shard_map/while/body/eval_jaxpr/slice | solution.py:24
  174.4 4.6 %copy.136 = bf16[6,8,128,640]{3,2,1,0:T(8,128)(2,1)} copy(bf16[6,8,128,640]{3,1,2,0:T(8,128)(2,1)S(1)} %bitcast.72) | data formatting | bytes 15728640 | tf_op jit(solution)/shard_map/while
  178.9 3.7 %fusion.78 = (bf16[16,3,128,128]{3,2,0,1:T(8,128)(2,1)S(1)}, bf16[16,3,128,128]{3,2,0,1:T(8,128)(2,1)S(1)}, bf16[16,3,128,128]{3,2,0,1:T(8,128)(2,1)S(1)}, bf16[...) fusion(bf16[16,3,128,640]{3,2,0,1:T(8,128)(2,1)} %bitcast.73), kind=kLoop, calls=%fused_computation.70.clone.1 | loop fusion | bytes 15728640 | tf_op jit(solution)/shard_map/while/body/eval_jaxpr/slice | solution.py:58
  188.3 35.3 %while.14 = (s32[]{:T(128)}, f32[16,1024]{1,0:T(8,128)S(1)}, s32[16,2]{0,1:T(2,128)S(1)}, f32[16,768]{1,0:T(8,128)S(1)}, s32[]{:T(128)}, /*index=5*/s32[]{:T(128)}) while((s32[]{:T(128)}, f32[16,1024]{1,0:T(8,128)S(1)}, s32[16,2]{0,1:T(2,128)S(1)}, f32[16,768]{1,0:T(8,128)S(1)}, s32[]{:T(128)}, /*index=5*/s32[]{:T(128)}) %tuple.55), condition=%wide.while_cond, body=%wide.while_body.sunk | while | flops 2 | bytes 12401 | solution.py:66
  189.0 1.5 dynamic-slice.7
  191.2 1.5 dynamic-slice.7
  193.4 1.5 dynamic-slice.7
  195.6 1.5 dynamic-slice.7
  197.8 1.5 dynamic-slice.7
  200.0 1.5 dynamic-slice.7
  202.2 1.5 dynamic-slice.7
  204.4 1.5 dynamic-slice.7
  206.6 1.5 dynamic-slice.7
  208.8 1.5 dynamic-slice.7
  211.0 1.5 dynamic-slice.7
  213.2 1.5 dynamic-slice.7
  215.4 1.5 dynamic-slice.7
  217.7 1.5 dynamic-slice.7
  219.9 1.5 dynamic-slice.7
  226.1 4.3 %tile.11 = bf16[16,3,128,641]{3,2,0,1:T(8,128)(2,1)} broadcast(bf16[16,3,641]{2,0,1:T(8,128)(2,1)S(1)} %concatenate.21), dimensions={0,1,3} | broadcast | bytes 7938144 | tf_op jit(solution)/shard_map/while/body/eval_jaxpr/tile | solution.py:23
  230.4 14.9 %tile.12 = bf16[16,3,82048]{2,0,1:T(8,128)(2,1)} reshape(bf16[16,3,128,641]{3,2,0,1:T(8,128)(2,1)} %tile.11) | data formatting | bytes 15753216 | tf_op jit(solution)/shard_map/while/body/eval_jaxpr/tile | solution.py:23
  245.3 3.2 %slice-done = bf16[16,3,81920]{2,0,1:T(8,128)(2,1)S(1)} async-done(((bf16[16,3,82048]{2,0,1:T(8,128)(2,1)}), bf16[16,3,81920]{2,0,1:T(8,128)(2,1)S(1)}, s32[]{:S(2)}) %slice-start) | async-done | bytes 7864344 | tf_op jit(solution)/shard_map/while/body/eval_jaxpr/slice | solution.py:24
  248.5 4.6 %copy.136 = bf16[6,8,128,640]{3,2,1,0:T(8,128)(2,1)} copy(bf16[6,8,128,640]{3,1,2,0:T(8,128)(2,1)S(1)} %bitcast.72) | data formatting | bytes 15728640 | tf_op jit(solution)/shard_map/while
  253.1 3.7 %fusion.78 = (bf16[16,3,128,128]{3,2,0,1:T(8,128)(2,1)S(1)}, bf16[16,3,128,128]{3,2,0,1:T(8,128)(2,1)S(1)}, bf16[16,3,128,128]{3,2,0,1:T(8,128)(2,1)S(1)}, bf16[...) fusion(bf16[16,3,128,640]{3,2,0,1:T(8,128)(2,1)} %bitcast.73), kind=kLoop, calls=%fused_computation.70.clone.1 | loop fusion | bytes 15728640 | tf_op jit(solution)/shard_map/while/body/eval_jaxpr/slice | solution.py:58
  262.4 35.3 %while.14 = (s32[]{:T(128)}, f32[16,1024]{1,0:T(8,128)S(1)}, s32[16,2]{0,1:T(2,128)S(1)}, f32[16,768]{1,0:T(8,128)S(1)}, s32[]{:T(128)}, /*index=5*/s32[]{:T(128)}) while((s32[]{:T(128)}, f32[16,1024]{1,0:T(8,128)S(1)}, s32[16,2]{0,1:T(2,128)S(1)}, f32[16,768]{1,0:T(8,128)S(1)}, s32[]{:T(128)}, /*index=5*/s32[]{:T(128)}) %tuple.55), condition=%wide.while_cond, body=%wide.while_body.sunk | while | flops 2 | bytes 12401 | solution.py:66
  263.1 1.5 dynamic-slice.7
  274.1 1.5 dynamic-slice.7
  294.0 1.5 dynamic-slice.7
  298.4 1.6 reshape_reshape.15
  300.0 6.9 %all-to-all-start.3 = ((f32[16,3,768]{2,1,0:T(4,128)}), f32[16,3,768]{2,1,0:T(4,128)S(1)}, u32[]{:S(2)}, u32[]{:S(2)}) async-start(f32[16,3,768]{2,1,0:T(4,128)} %reshape_reshape.15), calls=%async_computation.3 | async-start | bytes 393216 | tf_op jit(solution)/shard_map/all_to_all | solution.py:149
  306.9 7.6 %all-to-all-done.3 = f32[16,3,768]{2,1,0:T(4,128)S(1)} async-done(((f32[16,3,768]{2,1,0:T(4,128)}), f32[16,3,768]{2,1,0:T(4,128)S(1)}, u32[]{:S(2)}, u32[]{:S(2)}) %all-to-all-start.3) | async-done | bytes 147488 | tf_op jit(solution)/shard_map/all_to_all | solution.py:149
  (274 shorter events, 92.3 us)
Async XLA Ops:
  0.0 39.5 %copy-start = (bf16[2,12,3,400]{3,0,2,1:T(2,128)(2,1)S(1)}, bf16[2,12,3,400]{3,0,2,1:T(2,128)(2,1)}, u32[]{:S(2)}) copy-start(bf16[2,12,3,400]{3,0,2,1:T(2,128)(2,1)} %param.7) | copy-start | bytes 172804
  3.2 36.3 %all-to-all-start = ((s32[16,1,3]{2,1,0:T(1,128)}), s32[16,1,3]{2,1,0:T(1,128)S(1)}, u32[]{:S(2)}, u32[]{:S(2)}) async-start(s32[16,1,3]{2,1,0:T(1,128)} %bitcast.7), calls=%async_computation | async-start | bytes 16384 | tf_op jit(solution)/shard_map/all_to_all | solution.py:130
  39.6 13.2 %all-to-all-start.2 = ((s32[16,1,3]{2,1,0:T(1,128)}), s32[16,1,3]{2,1,0:T(1,128)S(1)}, u32[]{:S(2)}, u32[]{:S(2)}) async-start(s32[16,1,3]{2,1,0:T(1,128)} %bitcast.11), calls=%async_computation.2 | async-start | bytes 16384 | tf_op jit(solution)/shard_map/all_to_all | solution.py:131
  52.8 22.3 %all-to-all-start.1 = ((bf16[16,3,3,400]{3,1,2,0:T(4,128)(2,1)}), bf16[16,3,3,400]{3,1,2,0:T(4,128)(2,1)S(1)}, u32[]{:S(2)}, u32[]{:S(2)}) async-start(bf16[16,3,3,400]{3,1,2,0:T(4,128)(2,1)} %copy.70), calls=%async_computation.1 | async-start | bytes 393216 | tf_op jit(solution)/shard_map/all_to_all | solution.py:129
  97.0 3.2 %slice-start = ((bf16[16,3,82048]{2,0,1:T(8,128)(2,1)}), bf16[16,3,81920]{2,0,1:T(8,128)(2,1)S(1)}, s32[]{:S(2)}) async-start(bf16[16,3,82048]{2,0,1:T(8,128)(2,1)} %tile.12), calls=%async_computation.4 | async-start | bytes 15728640 | tf_op jit(solution)/shard_map/while/body/eval_jaxpr/slice | solution.py:24
  171.1 3.2 %slice-start = ((bf16[16,3,82048]{2,0,1:T(8,128)(2,1)}), bf16[16,3,81920]{2,0,1:T(8,128)(2,1)S(1)}, s32[]{:S(2)}) async-start(bf16[16,3,82048]{2,0,1:T(8,128)(2,1)} %tile.12), calls=%async_computation.4 | async-start | bytes 15728640 | tf_op jit(solution)/shard_map/while/body/eval_jaxpr/slice | solution.py:24
  245.3 3.2 %slice-start = ((bf16[16,3,82048]{2,0,1:T(8,128)(2,1)}), bf16[16,3,81920]{2,0,1:T(8,128)(2,1)S(1)}, s32[]{:S(2)}) async-start(bf16[16,3,82048]{2,0,1:T(8,128)(2,1)} %tile.12), calls=%async_computation.4 | async-start | bytes 15728640 | tf_op jit(solution)/shard_map/while/body/eval_jaxpr/slice | solution.py:24
  300.0 14.5 %all-to-all-start.3 = ((f32[16,3,768]{2,1,0:T(4,128)}), f32[16,3,768]{2,1,0:T(4,128)S(1)}, u32[]{:S(2)}, u32[]{:S(2)}) async-start(f32[16,3,768]{2,1,0:T(4,128)} %reshape_reshape.15), calls=%async_computation.3 | async-start | bytes 393216 | tf_op jit(solution)/shard_map/all_to_all | solution.py:149
where the time goes:
time: 318 us; the launch traced here: 316 us
  local copies, waits for them, and re-layouts  217 us (68%)
  blocking collectives  39.1 us (12%)
  starting transfers between devices  24.9 us (8%)
  matrix products  13.8 us (4%)
  waiting for transfers between devices  11.5 us (4%)
  other arithmetic  8.16 us (3%)
    gather x192, local copies, waits for them, and re-layouts  105 us
    another operation x6, local copies, waits for them, and re-layouts, toeplitz(): repeated = jnp.tile(padded, (1,) * len(leading) + (frame_size,))  57.4 us
    all_gather x1, blocking collectives, shards(): group_scale = lax.all_gather(local_scale, 'tp', axis=0, tiled=True)  22.2 us
    all_gather x1, blocking collectives, shards(): group_rows = lax.all_gather(continuous, 'tp', axis=0, tiled=True)  16.9 us
    dot_general x15, matrix products, correlate(): jnp.einsum('ncbp,ncip->ncbi', frames[:, :, step_index:step_index + blocks...  13.8 us
    while x9, local copies, waits for them, and re-layouts  13.8 us
    slice x3, local copies, waits for them, and re-layouts, correlate(): bands[..., step_index * frame_size:(step_index + 1) * frame_size]  11.2 us
    slice x6, local copies, waits for them, and re-layouts, toeplitz(): repeated[..., :frame_size * row_width]  9.7 us
  transfers between devices with their start and end apart: 4, of which 2 were waited for; matrix products, arithmetic and copies ran while one was open for 3% of the time, Pallas kernels for 0%

commit v1 on v0

--- a/solution.py
+++ b/solution.py
@@ -99,7 +99,9 @@
     flat_templates = templates.reshape(entries, CH, TLEN)
     group_rows = lax.all_gather(continuous, "tp", axis=0, tiled=True)
     local_scale = inverse_level(continuous)
-    group_scale = lax.all_gather(local_scale, "tp", axis=0, tiled=True)
+    group_scale = jnp.concatenate(
+        lax.all_to_all(jnp.stack([local_scale] * lax.axis_size("tp")), "tp", 0, 0), axis=0
+    )
     slot_templates = (
         jnp.zeros((slots_total, CH, TLEN), jnp.bfloat16)
         .at[slot_index]

time: 318 us -> 323 us (1.016)
  blocking collectives: 39.1 us -> 24.1 us
  waiting for transfers between devices: 11.5 us -> 21.1 us
  starting transfers between devices: 24.9 us -> 33.7 us
    all_gather x1 -> x0, blocking collectives: 22.2 us -> none  [shards(): group_scale = lax.all_gather(local_scale, 'tp', axis=0, tiled=True)]
    all_to_all x0 -> x1, starting transfers between devices: none -> 12.4 us  [shards(): lax.all_to_all(jnp.stack([local_scale] * lax.axis_size('tp')), 'tp', 0, 0)]
    all_gather x1, blocking collectives: 16.9 us -> 24.1 us  [shards(): group_rows = lax.all_gather(continuous, 'tp', axis=0, tiled=True)]
    all_to_all x1, waiting for transfers between devices: 0.01 us -> 7.12 us  [shards(): lax.all_to_all(slot_templates, 'st', split_axis=0, concat_axis=0, tiled=T...]
    all_to_all x1, starting transfers between devices: 6.85 us -> 3.52 us  [shards(): lax.all_to_all(aligned, 'st', split_axis=0, concat_axis=0, tiled=True)]
    while x9 -> x10, local copies, waits for them, and re-layouts: 13.8 us -> 14 us
  transfers between devices with their start and end apart: 4 -> 5, of which waited for: 2 -> 3; matrix products, arithmetic and copies ran while one was open for 3% -> 4% of each run, Pallas kernels for 0% -> 0%
where the time goes in v1:
time: 323 us; the launch traced here: 321 us
  local copies, waits for them, and re-layouts  218 us (67%)
  starting transfers between devices  33.7 us (10%)
  blocking collectives  24.1 us (7%)
  waiting for transfers between devices  21.1 us (7%)
  matrix products  13.8 us (4%)
  other arithmetic  8.41 us (3%)
    gather x192, local copies, waits for them, and re-layouts  105 us
    another operation x6, local copies, waits for them, and re-layouts, toeplitz(): repeated = jnp.tile(padded, (1,) * len(leading) + (frame_size,))  57.4 us
    all_gather x1, blocking collectives, shards(): group_rows = lax.all_gather(continuous, 'tp', axis=0, tiled=True)  24.1 us
    dot_general x15, matrix products, correlate(): jnp.einsum('ncbp,ncip->ncbi', frames[:, :, step_index:step_index + blocks...  13.8 us
    while x9, local copies, waits for them, and re-layouts  13.8 us
    all_to_all x1, starting transfers between devices, shards(): lax.all_to_all(jnp.stack([local_scale] * lax.axis_size('tp')), 'tp', 0, 0)  12.4 us
    slice x3, local copies, waits for them, and re-layouts, correlate(): bands[..., step_index * frame_size:(step_index + 1) * frame_size]  11.2 us
    slice x6, local copies, waits for them, and re-layouts, toeplitz(): repeated[..., :frame_size * row_width]  9.7 us
  transfers between devices with their start and end apart: 5, of which 3 were waited for; matrix products, arithmetic and copies ran while one was open for 4% of the time, Pallas kernels for 0%

profile of v1, /device:TPU:1, one launch (start us, length us, event | category | flops | bytes accessed | tf_op | source)
XLA Modules:
  0.0 320.7 jit_solution(4394900091623681980)
XLA Ops:
  3.2 7.6 %all-to-all-start = ((s32[16,1,3]{2,1,0:T(1,128)}), s32[16,1,3]{2,1,0:T(1,128)S(1)}, u32[]{:S(2)}, u32[]{:S(2)}) async-start(s32[16,1,3]{2,1,0:T(1,128)} %bitcast.7), calls=%async_computation | async-start | bytes 16384 | tf_op jit(solution)/shard_map/all_to_all | solution.py:132
  14.6 1.7 reduce-window.6
  17.3 1.5 scatter_fusion
  19.6 6.7 %all-to-all-start.3 = ((s32[16,1,3]{2,1,0:T(1,128)}), s32[16,1,3]{2,1,0:T(1,128)S(1)}, u32[]{:S(2)}, u32[]{:S(2)}) async-start(s32[16,1,3]{2,1,0:T(1,128)} %bitcast.12), calls=%async_computation.3 | async-start | bytes 16384 | tf_op jit(solution)/shard_map/all_to_all | solution.py:133
  26.4 6.1 %all-to-all-done.3 = s32[16,1,3]{2,1,0:T(1,128)S(1)} async-done(((s32[16,1,3]{2,1,0:T(1,128)}), s32[16,1,3]{2,1,0:T(1,128)S(1)}, u32[]{:S(2)}, u32[]{:S(2)}) %all-to-all-start.3) | async-done | bytes 224 | tf_op jit(solution)/shard_map/all_to_all | solution.py:133
  32.5 3.5 %all-to-all-start.1 = ((bf16[16,3,3,400]{3,1,2,0:T(4,128)(2,1)}), bf16[16,3,3,400]{3,1,2,0:T(4,128)(2,1)S(1)}, u32[]{:S(2)}, u32[]{:S(2)}) async-start(bf16[16,3,3,400]{3,1,2,0:T(4,128)(2,1)} %copy.96), calls=%async_computation.1 | async-start | bytes 393216 | tf_op jit(solution)/shard_map/all_to_all | solution.py:131
  36.2 7.1 %all-to-all-done.1 = bf16[16,3,3,400]{3,1,2,0:T(4,128)(2,1)S(1)} async-done(((bf16[16,3,3,400]{3,1,2,0:T(4,128)(2,1)}), bf16[16,3,3,400]{3,1,2,0:T(4,128)(2,1)S(1)}, u32[]{:S(2)}, u32[]{:S(2)}) %all-to-all-start.1) | async-done | bytes 115232 | tf_op jit(solution)/shard_map/all_to_all | solution.py:131
  44.1 12.4 %all-to-all-start.2 = ((f32[16,2,3,1024]{3,1,2,0:T(2,128)}), f32[16,2,3,1024]{3,1,2,0:T(2,128)S(1)}, u32[]{:S(2)}, u32[]{:S(2)}) async-start(f32[16,2,3,1024]{3,1,2,0:T(2,128)} %stack.2), calls=%async_computation.2 | async-start | bytes 786432 | tf_op jit(solution)/shard_map/all_to_all | solution.py:103
  56.5 24.1 %all_gather.3 = bf16[32,3,1424]{2,1,0:T(4,128)(2,1)S(1)} all-gather(bf16[2,3,1424]{2,1,0:T(4,128)(2,1)S(1)} %copy.93), channel_id=1, replica_groups=mesh['st'=16,'tp'=16] {'tp'}, dimensions={0}, use_global_device_ids=true | all-gather | bytes 290496 | tf_op jit(solution)/shard_map/all_gather | solution.py:100
  83.8 222.5 %while.13 = (s32[]{:T(128)}, f32[3,16,768]{2,1,0:T(8,128)}, s32[3,16]{1,0:T(4,128)S(1)}, bf16[32,3,1424]{2,1,0:T(4,128)(2,1)S(1)}, bf16[3,16,3,400]{3,1,0,2:T(8,...) while((s32[]{:T(128)}, f32[3,16,768]{2,1,0:T(8,128)}, ...), condition=%wide.region_10.11_spmd, body=%wide.region_7.10_spmd.sunk | while | flops 63301088 | bytes 91004616 | solution.py:77
  85.8 4.3 %tile.11 = bf16[16,3,128,641]{3,2,0,1:T(8,128)(2,1)} broadcast(bf16[16,3,641]{2,0,1:T(8,128)(2,1)S(1)} %concatenate.21), dimensions={0,1,3} | broadcast | bytes 7938144 | tf_op jit(solution)/shard_map/while/body/eval_jaxpr/tile | solution.py:23
  90.0 14.9 %tile.12 = bf16[16,3,82048]{2,0,1:T(8,128)(2,1)} reshape(bf16[16,3,128,641]{3,2,0,1:T(8,128)(2,1)} %tile.11) | data formatting | bytes 15753216 | tf_op jit(solution)/shard_map/while/body/eval_jaxpr/tile | solution.py:23
  104.9 3.2 %slice-done = bf16[16,3,81920]{2,0,1:T(8,128)(2,1)S(1)} async-done(((bf16[16,3,82048]{2,0,1:T(8,128)(2,1)}), bf16[16,3,81920]{2,0,1:T(8,128)(2,1)S(1)}, s32[]{:S(2)}) %slice-start) | async-done | bytes 7864344 | tf_op jit(solution)/shard_map/while/body/eval_jaxpr/slice | solution.py:24
  108.2 4.6 %copy.165 = bf16[6,8,128,640]{3,2,1,0:T(8,128)(2,1)} copy(bf16[6,8,128,640]{3,1,2,0:T(8,128)(2,1)S(1)} %bitcast.73) | data formatting | bytes 15728640 | tf_op jit(solution)/shard_map/while
  112.7 3.7 %fusion.78 = (bf16[16,3,128,128]{3,2,0,1:T(8,128)(2,1)S(1)}, bf16[16,3,128,128]{3,2,0,1:T(8,128)(2,1)S(1)}, bf16[16,3,128,128]{3,2,0,1:T(8,128)(2,1)S(1)}, bf16[...) fusion(bf16[16,3,128,640]{3,2,0,1:T(8,128)(2,1)} %bitcast.74), kind=kLoop, calls=%fused_computation.70.clone.1 | loop fusion | bytes 15728640 | tf_op jit(solution)/shard_map/while/body/eval_jaxpr/slice | solution.py:58
  122.1 35.3 %while.14 = (s32[]{:T(128)}, f32[16,1024]{1,0:T(8,128)S(1)}, s32[16,2]{0,1:T(2,128)S(1)}, f32[16,768]{1,0:T(8,128)S(1)}, s32[]{:T(128)}, /*index=5*/s32[]{:T(128)}) while((s32[]{:T(128)}, f32[16,1024]{1,0:T(8,128)S(1)}, s32[16,2]{0,1:T(2,128)S(1)}, f32[16,768]{1,0:T(8,128)S(1)}, s32[]{:T(128)}, /*index=5*/s32[]{:T(128)}) %tuple.56), condition=%wide.while_cond, body=%wide.while_body.sunk | while | flops 2 | bytes 12401 | solution.py:66
  122.8 1.5 dynamic-slice.7
  125.0 1.5 dynamic-slice.7
  127.2 1.5 dynamic-slice.7
  129.4 1.5 dynamic-slice.7
  131.6 1.5 dynamic-slice.7
  133.8 1.5 dynamic-slice.7
  136.0 1.5 dynamic-slice.7
  138.2 1.5 dynamic-slice.7
  140.4 1.5 dynamic-slice.7
  142.6 1.5 dynamic-slice.7
  144.8 1.5 dynamic-slice.7
  147.0 1.5 dynamic-slice.7
  149.3 1.5 dynamic-slice.7
  151.5 1.5 dynamic-slice.7
  153.7 1.5 dynamic-slice.7
  155.9 1.5 dynamic-slice.7
  159.9 4.3 %tile.11 = bf16[16,3,128,641]{3,2,0,1:T(8,128)(2,1)} broadcast(bf16[16,3,641]{2,0,1:T(8,128)(2,1)S(1)} %concatenate.21), dimensions={0,1,3} | broadcast | bytes 7938144 | tf_op jit(solution)/shard_map/while/body/eval_jaxpr/tile | solution.py:23
  164.2 14.9 %tile.12 = bf16[16,3,82048]{2,0,1:T(8,128)(2,1)} reshape(bf16[16,3,128,641]{3,2,0,1:T(8,128)(2,1)} %tile.11) | data formatting | bytes 15753216 | tf_op jit(solution)/shard_map/while/body/eval_jaxpr/tile | solution.py:23
  179.1 3.2 %slice-done = bf16[16,3,81920]{2,0,1:T(8,128)(2,1)S(1)} async-done(((bf16[16,3,82048]{2,0,1:T(8,128)(2,1)}), bf16[16,3,81920]{2,0,1:T(8,128)(2,1)S(1)}, s32[]{:S(2)}) %slice-start) | async-done | bytes 7864344 | tf_op jit(solution)/shard_map/while/body/eval_jaxpr/slice | solution.py:24
  182.3 4.6 %copy.165 = bf16[6,8,128,640]{3,2,1,0:T(8,128)(2,1)} copy(bf16[6,8,128,640]{3,1,2,0:T(8,128)(2,1)S(1)} %bitcast.73) | data formatting | bytes 15728640 | tf_op jit(solution)/shard_map/while
  186.9 3.7 %fusion.78 = (bf16[16,3,128,128]{3,2,0,1:T(8,128)(2,1)S(1)}, bf16[16,3,128,128]{3,2,0,1:T(8,128)(2,1)S(1)}, bf16[16,3,128,128]{3,2,0,1:T(8,128)(2,1)S(1)}, bf16[...) fusion(bf16[16,3,128,640]{3,2,0,1:T(8,128)(2,1)} %bitcast.74), kind=kLoop, calls=%fused_computation.70.clone.1 | loop fusion | bytes 15728640 | tf_op jit(solution)/shard_map/while/body/eval_jaxpr/slice | solution.py:58
  196.2 35.3 %while.14 = (s32[]{:T(128)}, f32[16,1024]{1,0:T(8,128)S(1)}, s32[16,2]{0,1:T(2,128)S(1)}, f32[16,768]{1,0:T(8,128)S(1)}, s32[]{:T(128)}, /*index=5*/s32[]{:T(128)}) while((s32[]{:T(128)}, f32[16,1024]{1,0:T(8,128)S(1)}, s32[16,2]{0,1:T(2,128)S(1)}, f32[16,768]{1,0:T(8,128)S(1)}, s32[]{:T(128)}, /*index=5*/s32[]{:T(128)}) %tuple.56), condition=%wide.while_cond, body=%wide.while_body.sunk | while | flops 2 | bytes 12401 | solution.py:66
  196.9 1.5 dynamic-slice.7
  199.1 1.5 dynamic-slice.7
  201.3 1.5 dynamic-slice.7
  203.5 1.5 dynamic-slice.7
  205.8 1.5 dynamic-slice.7
  208.0 1.5 dynamic-slice.7
  210.2 1.5 dynamic-slice.7
  212.4 1.5 dynamic-slice.7
  214.6 1.5 dynamic-slice.7
  216.8 1.5 dynamic-slice.7
  219.0 1.5 dynamic-slice.7
  221.2 1.5 dynamic-slice.7
  223.4 1.5 dynamic-slice.7
  227.8 1.5 dynamic-slice.7
  234.1 4.3 %tile.11 = bf16[16,3,128,641]{3,2,0,1:T(8,128)(2,1)} broadcast(bf16[16,3,641]{2,0,1:T(8,128)(2,1)S(1)} %concatenate.21), dimensions={0,1,3} | broadcast | bytes 7938144 | tf_op jit(solution)/shard_map/while/body/eval_jaxpr/tile | solution.py:23
  238.3 14.9 %tile.12 = bf16[16,3,82048]{2,0,1:T(8,128)(2,1)} reshape(bf16[16,3,128,641]{3,2,0,1:T(8,128)(2,1)} %tile.11) | data formatting | bytes 15753216 | tf_op jit(solution)/shard_map/while/body/eval_jaxpr/tile | solution.py:23
  253.2 3.2 %slice-done = bf16[16,3,81920]{2,0,1:T(8,128)(2,1)S(1)} async-done(((bf16[16,3,82048]{2,0,1:T(8,128)(2,1)}), bf16[16,3,81920]{2,0,1:T(8,128)(2,1)S(1)}, s32[]{:S(2)}) %slice-start) | async-done | bytes 7864344 | tf_op jit(solution)/shard_map/while/body/eval_jaxpr/slice | solution.py:24
  256.5 4.6 %copy.165 = bf16[6,8,128,640]{3,2,1,0:T(8,128)(2,1)} copy(bf16[6,8,128,640]{3,1,2,0:T(8,128)(2,1)S(1)} %bitcast.73) | data formatting | bytes 15728640 | tf_op jit(solution)/shard_map/while
  261.0 3.7 %fusion.78 = (bf16[16,3,128,128]{3,2,0,1:T(8,128)(2,1)S(1)}, bf16[16,3,128,128]{3,2,0,1:T(8,128)(2,1)S(1)}, bf16[16,3,128,128]{3,2,0,1:T(8,128)(2,1)S(1)}, bf16[...) fusion(bf16[16,3,128,640]{3,2,0,1:T(8,128)(2,1)} %bitcast.74), kind=kLoop, calls=%fused_computation.70.clone.1 | loop fusion | bytes 15728640 | tf_op jit(solution)/shard_map/while/body/eval_jaxpr/slice | solution.py:58
  270.4 35.3 %while.14 = (s32[]{:T(128)}, f32[16,1024]{1,0:T(8,128)S(1)}, s32[16,2]{0,1:T(2,128)S(1)}, f32[16,768]{1,0:T(8,128)S(1)}, s32[]{:T(128)}, /*index=5*/s32[]{:T(128)}) while((s32[]{:T(128)}, f32[16,1024]{1,0:T(8,128)S(1)}, s32[16,2]{0,1:T(2,128)S(1)}, f32[16,768]{1,0:T(8,128)S(1)}, s32[]{:T(128)}, /*index=5*/s32[]{:T(128)}) %tuple.56), condition=%wide.while_cond, body=%wide.while_body.sunk | while | flops 2 | bytes 12401 | solution.py:66
  282.1 1.5 dynamic-slice.7
  293.1 1.5 dynamic-slice.7
  304.2 1.5 dynamic-slice.7
  306.3 1.6 reshape_reshape.15
  308.0 3.5 %all-to-all-start.4 = ((f32[16,3,768]{2,1,0:T(4,128)}), f32[16,3,768]{2,1,0:T(4,128)S(1)}, u32[]{:S(2)}, u32[]{:S(2)}) async-start(f32[16,3,768]{2,1,0:T(4,128)} %reshape_reshape.15), calls=%async_computation.4 | async-start | bytes 393216 | tf_op jit(solution)/shard_map/all_to_all | solution.py:151
  311.5 7.9 %all-to-all-done.4 = f32[16,3,768]{2,1,0:T(4,128)S(1)} async-done(((f32[16,3,768]{2,1,0:T(4,128)}), f32[16,3,768]{2,1,0:T(4,128)S(1)}, u32[]{:S(2)}, u32[]{:S(2)}) %all-to-all-start.4) | async-done | bytes 147488 | tf_op jit(solution)/shard_map/all_to_all | solution.py:151
  (276 shorter events, 95.2 us)
Async XLA Ops:
  3.2 16.4 %all-to-all-start = ((s32[16,1,3]{2,1,0:T(1,128)}), s32[16,1,3]{2,1,0:T(1,128)S(1)}, u32[]{:S(2)}, u32[]{:S(2)}) async-start(s32[16,1,3]{2,1,0:T(1,128)} %bitcast.7), calls=%async_computation | async-start | bytes 16384 | tf_op jit(solution)/shard_map/all_to_all | solution.py:132
  16.4 40.1 %copy-start = (bf16[2,3,1424]{2,0,1:T(2,128)(2,1)S(1)}, bf16[2,3,1424]{2,0,1:T(2,128)(2,1)}, u32[]{:S(2)}) copy-start(bf16[2,3,1424]{2,0,1:T(2,128)(2,1)} %param.6) | copy-start | bytes 51268
  19.6 12.9 %all-to-all-start.3 = ((s32[16,1,3]{2,1,0:T(1,128)}), s32[16,1,3]{2,1,0:T(1,128)S(1)}, u32[]{:S(2)}, u32[]{:S(2)}) async-start(s32[16,1,3]{2,1,0:T(1,128)} %bitcast.12), calls=%async_computation.3 | async-start | bytes 16384 | tf_op jit(solution)/shard_map/all_to_all | solution.py:133
  32.5 10.8 %all-to-all-start.1 = ((bf16[16,3,3,400]{3,1,2,0:T(4,128)(2,1)}), bf16[16,3,3,400]{3,1,2,0:T(4,128)(2,1)S(1)}, u32[]{:S(2)}, u32[]{:S(2)}) async-start(bf16[16,3,3,400]{3,1,2,0:T(4,128)(2,1)} %copy.96), calls=%async_computation.1 | async-start | bytes 393216 | tf_op jit(solution)/shard_map/all_to_all | solution.py:131
  44.1 39.5 %all-to-all-start.2 = ((f32[16,2,3,1024]{3,1,2,0:T(2,128)}), f32[16,2,3,1024]{3,1,2,0:T(2,128)S(1)}, u32[]{:S(2)}, u32[]{:S(2)}) async-start(f32[16,2,3,1024]{3,1,2,0:T(2,128)} %stack.2), calls=%async_computation.2 | async-start | bytes 786432 | tf_op jit(solution)/shard_map/all_to_all | solution.py:103
  104.9 3.2 %slice-start = ((bf16[16,3,82048]{2,0,1:T(8,128)(2,1)}), bf16[16,3,81920]{2,0,1:T(8,128)(2,1)S(1)}, s32[]{:S(2)}) async-start(bf16[16,3,82048]{2,0,1:T(8,128)(2,1)} %tile.12), calls=%async_computation.5 | async-start | bytes 15728640 | tf_op jit(solution)/shard_map/while/body/eval_jaxpr/slice | solution.py:24
  179.1 3.2 %slice-start = ((bf16[16,3,82048]{2,0,1:T(8,128)(2,1)}), bf16[16,3,81920]{2,0,1:T(8,128)(2,1)S(1)}, s32[]{:S(2)}) async-start(bf16[16,3,82048]{2,0,1:T(8,128)(2,1)} %tile.12), calls=%async_computation.5 | async-start | bytes 15728640 | tf_op jit(solution)/shard_map/while/body/eval_jaxpr/slice | solution.py:24
  253.2 3.2 %slice-start = ((bf16[16,3,82048]{2,0,1:T(8,128)(2,1)}), bf16[16,3,81920]{2,0,1:T(8,128)(2,1)S(1)}, s32[]{:S(2)}) async-start(bf16[16,3,82048]{2,0,1:T(8,128)(2,1)} %tile.12), calls=%async_computation.5 | async-start | bytes 15728640 | tf_op jit(solution)/shard_map/while/body/eval_jaxpr/slice | solution.py:24
  308.0 11.4 %all-to-all-start.4 = ((f32[16,3,768]{2,1,0:T(4,128)}), f32[16,3,768]{2,1,0:T(4,128)S(1)}, u32[]{:S(2)}, u32[]{:S(2)}) async-start(f32[16,3,768]{2,1,0:T(4,128)} %reshape_reshape.15), calls=%async_computation.4 | async-start | bytes 393216 | tf_op jit(solution)/shard_map/all_to_all | solution.py:151
